TPU v7x, 128 devices: a whole 4x4x4 slice. The times are simulated.
128 devices in a mesh: gr: 16 (over x, y), gc: 8 (over z, core).
Axes of the slice: x: 4, y: 4, z: 4, core: 2. Of those that a mesh axis runs over, the one named last changes fastest.
Arguments:
- child_rows: float32 [8192, 12288], P('gr', 'gc'), may hold values from -1.5 to 1.5
- row_map: int32 [8192], P('gr'), may hold values from 0 to 8191, as said below
- stair: int32 [64], replicated, may hold values from 0 to 896, as said below
Outputs:
- factor: float32 [1024, 12288], P('gr', 'gc')
- projected: float32 [8192, 12288], P('gr', 'gc')
Inputs may be any that keep to these rules, and one draw needn't show every extreme that they name: row_map is a permutation of 0 to 8191. Of the 512 rows of one index of gr, at most 152 go to the rows of any one index of gr (row_map // 512), and some index of gr sends exactly 152 to one index. stair is nondecreasing and a multiple of 128; the first quarter of the blocks is 0 and the last block holds 896.
All inputs are finite; a program needn't handle non-finite values.
Results may differ from a plain program's by a relative error of at most 0.0003.
Values sent between devices are 32-bit elements; how exact they have to be, the bound alone decides.
A program may use at most 128 MiB of HBM per device.

v0:
```python
import jax
import jax.numpy as jnp
from jax import lax
from jax.sharding import PartitionSpec as P

PANEL = 512
NPANEL = 2
STAIR_BLOCK = 128


def spread(value, axis, source):
    kept = jnp.where(lax.axis_index(axis) == source, value, 0).astype(value.dtype)
    return lax.psum(kept, axis)


def pack_rows(values, targets, groups):
    rows_dev = values.shape[0]
    base_rows = 3 * rows_dev // (4 * groups)
    capacity = rows_dev - base_rows * (groups - 1)
    target_dev = targets // rows_dev
    target_row = targets % rows_dev
    onehot = (target_dev[:, None] == jnp.arange(groups, dtype=jnp.int32)[None, :]).astype(jnp.int32)
    rank_within = jnp.sum((jnp.cumsum(onehot, axis=0) - onehot) * onehot, axis=1)
    buffer_index = target_dev * capacity + rank_within
    source_row = (
        jnp.full((groups * capacity,), rows_dev, jnp.int32)
        .at[buffer_index]
        .set(jnp.arange(rows_dev, dtype=jnp.int32))
    )
    sent_rows = jnp.take(values, source_row, axis=0, mode="fill", fill_value=0.0)
    sent_slots = (
        jnp.full((groups * capacity,), rows_dev, jnp.int32).at[buffer_index].set(target_row)
    )
    return (
        sent_rows.reshape(groups, capacity, values.shape[1]),
        sent_slots.reshape(groups, capacity),
    )


def place_rows(recv_rows, recv_slots, rows_dev):
    flat_rows = recv_rows.reshape(-1, recv_rows.shape[-1])
    flat_slots = recv_slots.reshape(-1)
    where_from = (
        jnp.zeros((rows_dev,), jnp.int32)
        .at[flat_slots]
        .set(jnp.arange(flat_slots.shape[0], dtype=jnp.int32), mode="drop")
    )
    return jnp.take(flat_rows, where_from, axis=0)


def matmul(left, right):
    return jnp.dot(left, right, precision=lax.Precision.HIGHEST, preferred_element_type=jnp.float32)


def shards(child_rows, row_map, stair):
    groups = lax.axis_size("gr")
    rows_dev, cols_dev = child_rows.shape
    columns = lax.axis_index("gc") * cols_dev + jnp.arange(cols_dev, dtype=jnp.int32)
    sent_rows, sent_slots = pack_rows(child_rows, row_map, groups)
    recv_rows, recv_slots = (
        lax.all_to_all(sent_rows, "gr", split_axis=0, concat_axis=0, tiled=True),
        lax.all_to_all(sent_slots, "gr", split_axis=0, concat_axis=0, tiled=True),
    )
    front_work = place_rows(recv_rows, recv_slots, rows_dev)
    own_rows = lax.axis_index("gr") * rows_dev + jnp.arange(rows_dev, dtype=jnp.int32)
    limits = jnp.take(stair, own_rows // STAIR_BLOCK)
    front_work = jnp.where(
        columns[None, :] >= limits[:, None], front_work, jnp.zeros_like(front_work)
    )
    blocks = []
    for step in range(NPANEL):
        panel_block = spread(front_work[:, step * PANEL : (step + 1) * PANEL], "gc", 0)
        gram_one = lax.psum(matmul(panel_block.T, panel_block), "gr")
        lower_one = jnp.linalg.cholesky(gram_one)
        basis_cols = jax.scipy.linalg.solve_triangular(lower_one, panel_block.T, lower=True).T
        coupling = lax.psum(matmul(basis_cols.T, front_work), "gr")
        front_work = front_work - matmul(basis_cols, coupling)
        blocks.append(coupling)
    stacked = jnp.concatenate(blocks, axis=0)
    share_rows = stacked.shape[0] // groups
    factor = lax.dynamic_slice_in_dim(stacked, lax.axis_index("gr") * share_rows, share_rows, 0)
    return (factor, front_work)


def solution(mesh):
    placed = (P("gr", "gc"), P("gr"), P())
    return jax.shard_map(
        shards,
        mesh=mesh,
        in_specs=placed,
        out_specs=(P("gr", "gc"), P("gr", "gc")),
        check_vma=False,
    )
```

profile of v0, /device:TPU:1, one launch (start us, length us, event | category | flops | bytes accessed | tf_op | source)
XLA Modules:
  0.0 1196.0 jit_solution(4208776243515195790)
XLA Ops:
  9.6 2.5 scatter_custom_fusion
  12.7 7.6 all-to-all-start
  20.3 2.5 scatter_custom_fusion.2
  23.0 10.1 gather_fusion
  33.1 11.6 broadcast_select_fusion
  44.7 6.8 all-to-all-start.1
  54.2 4.4 compare_select_fusion.3
  60.1 35.7 %select_select_fusion.3 = s32[512]{0:T(512)S(1)} fusion(pred[512]{0:T(512)(128)(4,1)S(1)} %get-tuple-element.130, pred[512]{0:T(512)(128)(4,1)S(1)} %get-tuple-element.131, pred[512]{0:T(512)(128)(4,1)S(1)} %get-tuple-element.132, pred[512]{0:T(512)(128)(4,1)S(1)} %get-tuple-element.133, pred[512]{0:T(512)(128)(4,1)S(1)} %get-tuple-element.134, ...), kind=kLoop, calls=%fused_computation.224 | loop fusion | flops 40960 | bytes 33512 | tf_op jit(solution)/shard_map/jit(_take)/select_n | solution.py:66
  96.0 12.3 %scatter_custom_fusion.1 = s32[512]{0:T(512)S(1)} fusion(s32[2432]{0:T(1024)S(1)} %fusion.63, s32[2432]{0:T(1024)S(1)} %iota.86, s32[]{:T(128)} %constant.193.clone.1), kind=kCustom, calls=%fused_computation.249 | custom fusion | bytes 2052 | tf_op jit(solution)/shard_map/scatter | solution.py:46
  108.4 204.8 %all-to-all-done.1 = f32[16,152,1536]{2,1,0:T(8,128)} async-done(((f32[16,152,1536]{2,1,0:T(8,128)}), f32[16,152,1536]{2,1,0:T(8,128)}, u32[]{:S(2)}, u32[]{:S(2)}) %all-to-all-start.1) | async-done | bytes 14942240 | tf_op jit(solution)/shard_map/all_to_all | solution.py:61
  313.2 9.8 gather_fusion.1
  323.0 2.3 select_select_fusion
  326.5 69.1 %all-reduce.8.cloned.1.call-done = f32[512,512]{1,0:T(8,128)} async-done(((f32[512,512]{1,0:T(8,128)}), f32[512,512]{1,0:T(8,128)}) %all-reduce.8.cloned.1.call-update) | async-done | bytes 1048592 | tf_op jit(solution)/shard_map/psum | solution.py:13
  395.6 4.4 fusion.88
  400.5 86.2 %all-reduce.10.cloned.1.call-done = f32[512,512]{0,1:T(8,128)} async-done(((f32[512,512]{0,1:T(8,128)}), f32[512,512]{0,1:T(8,128)}) %all-reduce.10.cloned.1.call-update) | async-done | bytes 1048592 | tf_op jit(solution)/shard_map/psum | solution.py:73
  486.7 2.5 copy.11
  492.0 11.7 cholesky.286
  504.9 9.8 custom-call.27
  517.9 11.7 cholesky.305
  530.3 10.0 custom-call.28
  542.6 11.7 cholesky.326
  554.9 9.8 custom-call.29
  567.0 11.7 cholesky.343
  584.6 2.7 select_select_fusion.2
  587.3 11.7 while.4
  599.0 39.9 %custom-call.30 = f32[4,128,128]{1,2,0:T(8,128)} custom-call(f32[4,128,128]{2,1,0:T(8,128)S(1)} %get-tuple-element.18), custom_call_target="InvertDiagBlocksLowerTriangular" | custom-call | tf_op jit(solution)/shard_map/jit(_solve_triangular)/triangular_solve | solution.py:75
  645.9 2.6 convolution_subtract_fusion.7
  649.7 6.9 fusion.13
  656.6 96.0 %all-reduce.12.cloned.1.call-done = f32[512,1536]{1,0:T(8,128)} async-done(((f32[512,1536]{1,0:T(8,128)}), f32[512,1536]{1,0:T(8,128)}) %all-reduce.12.cloned.1.call-update) | async-done | bytes 3145744 | tf_op jit(solution)/shard_map/psum | solution.py:76
  752.6 7.8 convolution_subtract_fusion.1
  761.7 60.2 %all-reduce.14.cloned.1.call-done = f32[512,512]{1,0:T(8,128)} async-done(((f32[512,512]{1,0:T(8,128)}), f32[512,512]{1,0:T(8,128)}) %all-reduce.14.cloned.1.call-update) | async-done | bytes 1048592 | tf_op jit(solution)/shard_map/psum | solution.py:13
  821.9 4.5 fusion.89
  826.7 86.5 %all-reduce.16.cloned.1.call-done = f32[512,512]{0,1:T(8,128)} async-done(((f32[512,512]{0,1:T(8,128)}), f32[512,512]{0,1:T(8,128)}) %all-reduce.16.cloned.1.call-update) | async-done | bytes 1048592 | tf_op jit(solution)/shard_map/psum | solution.py:73
  913.1 2.5 copy.13
  918.4 11.7 cholesky.358
  931.3 9.8 custom-call.31
  944.3 11.7 cholesky.377
  956.6 10.0 custom-call.32
  969.0 11.7 cholesky.398
  981.3 9.8 custom-call.33
  993.4 11.7 cholesky.415
  1011.0 2.7 select_select_fusion.1
  1013.8 11.8 while.5
  1025.5 39.9 %custom-call.34 = f32[4,128,128]{1,2,0:T(8,128)} custom-call(f32[4,128,128]{2,1,0:T(8,128)S(1)} %get-tuple-element.19), custom_call_target="InvertDiagBlocksLowerTriangular" | custom-call | tf_op jit(solution)/shard_map/jit(_solve_triangular)/triangular_solve | solution.py:75
  1072.4 2.6 convolution_subtract_fusion.6
  1076.2 6.9 fusion.12
  1083.1 95.9 %all-reduce.18.cloned.1.call-done = f32[512,1536]{1,0:T(8,128)} async-done(((f32[512,1536]{1,0:T(8,128)}), f32[512,1536]{1,0:T(8,128)}) %all-reduce.18.cloned.1.call-update) | async-done | bytes 3145744 | tf_op jit(solution)/shard_map/psum | solution.py:76
  1179.0 9.2 convolution_subtract_fusion
  (183 shorter events, 83.5 us)
Async XLA Ops:
  7.2 15.8 %copy-start = (f32[512,1536]{1,0:T(8,128)S(1)}, f32[512,1536]{1,0:T(8,128)}, u32[]{:S(2)}) copy-start(f32[512,1536]{1,0:T(8,128)} %param.6) | copy-start | bytes 9437188
  12.7 32.0 %all-to-all-start = ((s32[16,1,152]{2,1,0:T(1,128)}), s32[16,1,152]{2,1,0:T(1,128)S(1)}, u32[]{:S(2)}, u32[]{:S(2)}) async-start(s32[16,1,152]{2,1,0:T(1,128)} %all_to_all.9), calls=%async_computation | async-start | bytes 32768 | tf_op jit(solution)/shard_map/all_to_all | solution.py:62
  44.7 8.1 copy-start.14
  44.7 268.5 %all-to-all-start.1 = ((f32[16,152,1536]{2,1,0:T(8,128)}), f32[16,152,1536]{2,1,0:T(8,128)}, u32[]{:S(2)}, u32[]{:S(2)}) async-start(f32[16,152,1536]{2,1,0:T(8,128)} %broadcast_select_fusion), calls=%async_computation.1 | async-start | bytes 29884416 | tf_op jit(solution)/shard_map/all_to_all | solution.py:61
  51.5 344.0 %all-reduce.8.cloned.1.call-start = ((), (), s32[]{:S(2)}) async-start(), calls=%async_computation.2 | async-start | bytes 2097152 | tf_op jit(solution)/shard_map/psum | solution.py:13
  325.3 323.6 %copy-start.3 = (f32[512,1536]{1,0:T(8,128)}, f32[512,1536]{1,0:T(8,128)S(1)}, u32[]{:S(2)}) copy-start(f32[512,1536]{1,0:T(8,128)S(1)} %select_select_fusion) | copy-start | bytes 9437188
  326.5 160.2 %all-reduce.10.cloned.1.call-start = ((), (), s32[]{:S(2)}) async-start(), calls=%async_computation.3 | async-start | bytes 2097152 | tf_op jit(solution)/shard_map/psum | solution.py:73
  400.0 352.6 %all-reduce.12.cloned.1.call-start = ((), (), s32[]{:S(2)}) async-start(), calls=%async_computation.4 | async-start | bytes 6291456 | tf_op jit(solution)/shard_map/psum | solution.py:76
  491.0 1.0 copy-start.10
  639.0 6.4 copy-start.15
  643.3 5.6 copy-start.7
  645.9 3.1 copy-start.9
  648.9 0.7 copy-start.13
  656.6 165.3 %all-reduce.14.cloned.1.call-start = ((), (), s32[]{:S(2)}) async-start(), calls=%async_computation.5 | async-start | bytes 2097152 | tf_op jit(solution)/shard_map/psum | solution.py:13
  760.4 315.0 %copy-start.2 = (f32[512,1536]{1,0:T(8,128)}, f32[512,1536]{1,0:T(8,128)S(1)}, u32[]{:S(2)}) copy-start(f32[512,1536]{1,0:T(8,128)S(1)} %convolution_subtract_fusion.1) | copy-start | bytes 9437188
  761.6 151.5 %all-reduce.16.cloned.1.call-start = ((), (), s32[]{:S(2)}) async-start(), calls=%async_computation.6 | async-start | bytes 2097152 | tf_op jit(solution)/shard_map/psum | solution.py:73
  826.4 352.6 %all-reduce.18.cloned.1.call-start = ((), (), s32[]{:S(2)}) async-start(), calls=%async_computation.7 | async-start | bytes 6291456 | tf_op jit(solution)/shard_map/psum | solution.py:76
  917.4 1.0 copy-start.11
  1065.5 6.4 copy-start.16
  1069.8 5.6 copy-start.6
  1072.4 3.1 copy-start.8
  1075.5 0.7 copy-start.12
  1179.0 9.2 copy-start.4
  1179.0 9.2 copy-start.5
  1179.0 10.0 copy-start.1
Sparse Core Ops, SparseCore 0:
  326.6 68.9 all-reduce.7
  400.1 86.5 all-reduce.9
  656.7 95.8 all-reduce.11
  761.7 60.1 all-reduce.13
  826.6 86.5 all-reduce.15
  1083.2 95.7 all-reduce.17
where the time goes:
time: 1210 us; the launch traced here: 1200 us
  waiting for transfers between devices  699 us (58%)
  other arithmetic  312 us (26%)
  local copies, waits for them, and re-layouts  75.2 us (6%)
  matrix products  74.9 us (6%)
  between operations  20.1 us (2%)
  starting transfers between devices  15.3 us (1%)
    all_to_all x1, waiting for transfers between devices, shards(): lax.all_to_all(sent_rows, 'gr', split_axis=0, concat_axis=0, tiled=True)  205 us
    psum x2, waiting for transfers between devices, shards(): coupling = lax.psum(matmul(basis_cols.T, front_work), 'gr')  192 us
    psum x2, waiting for transfers between devices, shards(): gram_one = lax.psum(matmul(panel_block.T, panel_block), 'gr')  173 us
    another operation x30, other arithmetic, shards(): lower_one = jnp.linalg.cholesky(gram_one)  162 us
    psum x2, waiting for transfers between devices, spread(): return lax.psum(kept, axis)  129 us
    another operation x5, other arithmetic, shards(): jax.scipy.linalg.solve_triangular(lower_one, panel_block.T, lower=True)  85.3 us
    dot_general x6, matrix products, matmul(): jnp.dot(left, right, precision=lax.Precision.HIGHEST, preferred_element_t...  39.7 us
    select_n x1, other arithmetic, shards(): limits = jnp.take(stair, own_rows // STAIR_BLOCK)  35.7 us
  transfers between devices with their start and end apart: 8, of which 7 were waited for; matrix products, arithmetic and copies ran while one was open for 7% of the time, Pallas kernels for 0%

commit v1 on v0

--- a/solution.py
+++ b/solution.py
@@ -73,7 +73,7 @@
         gram_one = lax.psum(matmul(panel_block.T, panel_block), "gr")
         lower_one = jnp.linalg.cholesky(gram_one)
         basis_cols = jax.scipy.linalg.solve_triangular(lower_one, panel_block.T, lower=True).T
-        coupling = lax.psum(matmul(basis_cols.T, front_work), "gr")
+        coupling = jnp.sum(lax.all_gather(matmul(basis_cols.T, front_work), "gr"), axis=0)
         front_work = front_work - matmul(basis_cols, coupling)
         blocks.append(coupling)
     stacked = jnp.concatenate(blocks, axis=0)

time: 1210 us -> 1620 us (1.34)
  waiting for transfers between devices: 699 us -> 1070 us
  other arithmetic: 312 us -> 352 us
    all_gather x0 -> x2, waiting for transfers between devices: none -> 567 us  [shards(): lax.all_gather(matmul(basis_cols.T, front_work), 'gr')]
    psum x2 -> x0, waiting for transfers between devices: 192 us -> none  [shards(): coupling = lax.psum(matmul(basis_cols.T, front_work), 'gr')]
    reduce_sum x0 -> x2, other arithmetic: none -> 41.2 us  [shards(): jnp.sum(lax.all_gather(matmul(basis_cols.T, front_work), 'gr'), axis=0)]
  transfers between devices with their start and end apart: 8 -> 8, of which waited for: 7 -> 7; matrix products, arithmetic and copies ran while one was open for 7% -> 5% of each run, Pallas kernels for 0% -> 0%
where the time goes in v1:
time: 1620 us; the launch traced here: 1610 us
  waiting for transfers between devices  1070 us (66%)
  other arithmetic  352 us (22%)
  local copies, waits for them, and re-layouts  75.2 us (5%)
  matrix products  74.6 us (5%)
  between operations  20.4 us (1%)
    all_gather x2, waiting for transfers between devices, shards(): lax.all_gather(matmul(basis_cols.T, front_work), 'gr')  567 us
    all_to_all x1, waiting for transfers between devices, shards(): lax.all_to_all(sent_rows, 'gr', split_axis=0, concat_axis=0, tiled=True)  205 us
    psum x2, waiting for transfers between devices, shards(): gram_one = lax.psum(matmul(panel_block.T, panel_block), 'gr')  173 us
    another operation x30, other arithmetic, shards(): lower_one = jnp.linalg.cholesky(gram_one)  162 us
    psum x2, waiting for transfers between devices, spread(): return lax.psum(kept, axis)  130 us
    another operation x5, other arithmetic, shards(): jax.scipy.linalg.solve_triangular(lower_one, panel_block.T, lower=True)  84.9 us
    reduce_sum x2, other arithmetic, shards(): jnp.sum(lax.all_gather(matmul(basis_cols.T, front_work), 'gr'), axis=0)  41.2 us
    dot_general x6, matrix products, matmul(): jnp.dot(left, right, precision=lax.Precision.HIGHEST, preferred_element_t...  39.3 us
  transfers between devices with their start and end apart: 8, of which 7 were waited for; matrix products, arithmetic and copies ran while one was open for 5% of the time, Pallas kernels for 0%

profile of v1, /device:TPU:1, one launch (start us, length us, event | category | flops | bytes accessed | tf_op | source)
XLA Modules:
  0.0 1612.2 jit_solution(11178570193207657573)
XLA Ops:
  12.7 7.6 all-to-all-start
  20.3 2.5 scatter_custom_fusion.2
  23.0 10.1 gather_fusion
  33.1 11.6 broadcast_select_fusion
  44.7 6.8 all-to-all-start.1
  54.2 4.4 compare_select_fusion.3
  60.1 35.7 %select_select_fusion.3 = s32[512]{0:T(512)S(1)} fusion(pred[512]{0:T(512)(128)(4,1)S(1)} %get-tuple-element.130, pred[512]{0:T(512)(128)(4,1)S(1)} %get-tuple-element.131, pred[512]{0:T(512)(128)(4,1)S(1)} %get-tuple-element.132, pred[512]{0:T(512)(128)(4,1)S(1)} %get-tuple-element.133, pred[512]{0:T(512)(128)(4,1)S(1)} %get-tuple-element.134, ...), kind=kLoop, calls=%fused_computation.224 | loop fusion | flops 40960 | bytes 33512 | tf_op jit(solution)/shard_map/jit(_take)/select_n | solution.py:66
  96.0 12.3 scatter_custom_fusion.1
  108.4 204.8 %all-to-all-done.1 = f32[16,152,1536]{2,1,0:T(8,128)} async-done(((f32[16,152,1536]{2,1,0:T(8,128)}), f32[16,152,1536]{2,1,0:T(8,128)}, u32[]{:S(2)}, u32[]{:S(2)}) %all-to-all-start.1) | async-done | bytes 14942240 | tf_op jit(solution)/shard_map/all_to_all | solution.py:61
  313.2 9.8 gather_fusion.1
  326.5 69.1 %all-reduce.6.cloned.1.call-done = f32[512,512]{1,0:T(8,128)} async-done(((f32[512,512]{1,0:T(8,128)}), f32[512,512]{1,0:T(8,128)}) %all-reduce.6.cloned.1.call-update) | async-done | bytes 1048592 | tf_op jit(solution)/shard_map/psum | solution.py:13
  395.6 4.4 fusion.88
  400.2 86.4 %all-reduce.8.cloned.1.call-done = f32[512,512]{0,1:T(8,128)} async-done(((f32[512,512]{0,1:T(8,128)}), f32[512,512]{0,1:T(8,128)}) %all-reduce.8.cloned.1.call-update) | async-done | bytes 1048592 | tf_op jit(solution)/shard_map/psum | solution.py:73
  486.6 2.5 copy.11
  492.0 11.7 cholesky.286
  504.8 9.8 custom-call.27
  517.8 11.7 cholesky.305
  531.5 10.2 custom-call.28
  544.1 11.7 cholesky.326
  557.1 9.8 custom-call.29
  569.1 11.7 cholesky.343
  584.7 2.5 select_select_fusion.2
  587.2 11.7 while.4
  598.9 39.9 %custom-call.30 = f32[4,128,128]{1,2,0:T(8,128)} custom-call(f32[4,128,128]{2,1,0:T(8,128)S(1)} %get-tuple-element.18), custom_call_target="InvertDiagBlocksLowerTriangular" | custom-call | tf_op jit(solution)/shard_map/jit(_solve_triangular)/triangular_solve | solution.py:75
  645.8 2.6 convolution_subtract_fusion.7
  649.6 6.9 fusion.13
  656.5 283.5 %all-gather.5.cloned.1.call-done = f32[8192,1536]{1,0:T(8,128)} async-done(((f32[512,1536]{1,0:T(8,128)}), f32[8192,1536]{1,0:T(8,128)}) %all-gather.5.cloned.1.call-update) | async-done | bytes 50331664 | tf_op jit(solution)/shard_map/all_gather | solution.py:76
  940.1 20.4 %reduce_sum.28 = f32[512,1536]{1,0:T(8,128)} reduce(f32[16,512,1536]{2,1,0:T(8,128)} %bitcast.197, f32[]{:T(128)} %constant.211.clone.1), dimensions={0}, to_apply=%region_16.19 | reduce | flops 11796480 | bytes 53477380 | tf_op jit(solution)/shard_map/reduce_sum | solution.py:76
  960.5 7.8 convolution_subtract_fusion.1
  969.6 60.4 %all-reduce.10.cloned.1.call-done = f32[512,512]{1,0:T(8,128)} async-done(((f32[512,512]{1,0:T(8,128)}), f32[512,512]{1,0:T(8,128)}) %all-reduce.10.cloned.1.call-update) | async-done | bytes 1048592 | tf_op jit(solution)/shard_map/psum | solution.py:13
  1030.0 4.4 fusion.89
  1034.9 86.2 %all-reduce.12.cloned.1.call-done = f32[512,512]{0,1:T(8,128)} async-done(((f32[512,512]{0,1:T(8,128)}), f32[512,512]{0,1:T(8,128)}) %all-reduce.12.cloned.1.call-update) | async-done | bytes 1048592 | tf_op jit(solution)/shard_map/psum | solution.py:73
  1121.1 2.5 copy.13
  1126.5 11.7 cholesky.358
  1139.3 9.8 custom-call.31
  1152.3 11.7 cholesky.377
  1166.0 10.0 custom-call.32
  1178.3 11.7 cholesky.398
  1191.3 9.8 custom-call.33
  1203.4 11.7 cholesky.415
  1219.0 2.5 select_select_fusion.1
  1221.5 11.7 while.5
  1233.2 39.9 %custom-call.34 = f32[4,128,128]{1,2,0:T(8,128)} custom-call(f32[4,128,128]{2,1,0:T(8,128)S(1)} %get-tuple-element.19), custom_call_target="InvertDiagBlocksLowerTriangular" | custom-call | tf_op jit(solution)/shard_map/jit(_solve_triangular)/triangular_solve | solution.py:75
  1280.1 2.6 convolution_subtract_fusion.6
  1283.8 6.9 fusion.12
  1290.8 283.6 %all-gather.7.cloned.1.call-done = f32[8192,1536]{1,0:T(8,128)} async-done(((f32[512,1536]{1,0:T(8,128)}), f32[8192,1536]{1,0:T(8,128)}) %all-gather.7.cloned.1.call-update) | async-done | bytes 50331664 | tf_op jit(solution)/shard_map/all_gather | solution.py:76
  1574.3 20.7 %reduce_sum.29 = f32[512,1536]{1,0:T(8,128)} reduce(f32[16,512,1536]{2,1,0:T(8,128)} %bitcast.196, f32[]{:T(128)} %constant.211.clone.1), dimensions={0}, to_apply=%region_19.22 | reduce | flops 11796480 | bytes 53477380 | tf_op jit(solution)/shard_map/reduce_sum | solution.py:76
  1595.1 9.0 convolution_subtract_fusion
  (185 shorter events, 88.1 us)
Async XLA Ops:
  7.2 15.8 copy-start
  12.7 32.0 %all-to-all-start = ((s32[16,1,152]{2,1,0:T(1,128)}), s32[16,1,152]{2,1,0:T(1,128)S(1)}, u32[]{:S(2)}, u32[]{:S(2)}) async-start(s32[16,1,152]{2,1,0:T(1,128)} %all_to_all.9), calls=%async_computation | async-start | bytes 32768 | tf_op jit(solution)/shard_map/all_to_all | solution.py:62
  44.7 8.1 copy-start.14
  44.7 268.5 %all-to-all-start.1 = ((f32[16,152,1536]{2,1,0:T(8,128)}), f32[16,152,1536]{2,1,0:T(8,128)}, u32[]{:S(2)}, u32[]{:S(2)}) async-start(f32[16,152,1536]{2,1,0:T(8,128)} %broadcast_select_fusion), calls=%async_computation.1 | async-start | bytes 29884416 | tf_op jit(solution)/shard_map/all_to_all | solution.py:61
  51.5 344.0 %all-reduce.6.cloned.1.call-start = ((), (), s32[]{:S(2)}) async-start(), calls=%async_computation.2 | async-start | bytes 2097152 | tf_op jit(solution)/shard_map/psum | solution.py:13
  325.3 323.6 %copy-start.3 = (f32[512,1536]{1,0:T(8,128)}, f32[512,1536]{1,0:T(8,128)S(1)}, u32[]{:S(2)}) copy-start(f32[512,1536]{1,0:T(8,128)S(1)} %select_select_fusion) | copy-start | bytes 9437188
  326.5 160.2 %all-reduce.8.cloned.1.call-start = ((), (), s32[]{:S(2)}) async-start(), calls=%async_computation.3 | async-start | bytes 2097152 | tf_op jit(solution)/shard_map/psum | solution.py:73
  400.0 540.1 %all-gather.5.cloned.1.call-start = ((), (), s32[]{:S(2)}) async-start(), calls=%async_computation.6 | async-start | bytes 53477376 | tf_op jit(solution)/shard_map/all_gather | solution.py:76
  490.9 1.0 copy-start.10
  638.9 6.4 copy-start.15
  643.2 5.6 copy-start.7
  645.8 3.1 copy-start.9
  648.9 0.7 copy-start.13
  656.5 373.6 %all-reduce.10.cloned.1.call-start = ((), (), s32[]{:S(2)}) async-start(), calls=%async_computation.4 | async-start | bytes 2097152 | tf_op jit(solution)/shard_map/psum | solution.py:13
  968.3 314.8 %copy-start.2 = (f32[512,1536]{1,0:T(8,128)}, f32[512,1536]{1,0:T(8,128)S(1)}, u32[]{:S(2)}) copy-start(f32[512,1536]{1,0:T(8,128)S(1)} %convolution_subtract_fusion.1) | copy-start | bytes 9437188
  969.5 151.6 %all-reduce.12.cloned.1.call-start = ((), (), s32[]{:S(2)}) async-start(), calls=%async_computation.5 | async-start | bytes 2097152 | tf_op jit(solution)/shard_map/psum | solution.py:73
  1034.4 539.9 %all-gather.7.cloned.1.call-start = ((), (), s32[]{:S(2)}) async-start(), calls=%async_computation.7 | async-start | bytes 53477376 | tf_op jit(solution)/shard_map/all_gather | solution.py:76
  1125.4 1.0 copy-start.11
  1273.2 6.4 copy-start.16
  1277.5 5.6 copy-start.6
  1280.1 3.1 copy-start.8
  1283.1 0.7 copy-start.12
  1595.1 9.0 copy-start.4
  1595.1 9.0 copy-start.5
  1595.1 9.8 copy-start.1
Sparse Core Ops, SparseCore 0:
  326.6 68.9 all-reduce.5
  400.1 86.4 all-reduce.7
  656.6 283.4 all-gather.4
  969.7 60.3 all-reduce.9
  1034.6 86.5 all-reduce.11
  1290.9 283.4 all-gather.6
